TPU v7x, 32 devices: a whole 2x2x4 slice. The times are simulated.
32 devices in a mesh: groups: 2 (over y), ctx: 4 (over z), dom: 2 (over x), tp: 2 (over core).
Axes of the slice: x: 2, y: 2, z: 4, core: 2. Of those that a mesh axis runs over, the one named last changes fastest.
Arguments:
- queries: bfloat16 [8, 32, 8, 8, 128], P('groups', 'dom', 'tp'), parts along dimension 0, may hold values from -8 to 8
- prompt_cache: bfloat16 [4, 8192, 8, 128], P('groups', 'ctx', 'tp'), parts along dimension 0, may hold values from -8 to 8
- suffix_cache: bfloat16 [4, 32, 16, 8, 128], P('groups', 'dom', 'ctx', 'tp'), parts along dimension 0, may hold values from -8 to 8
- new_kv: bfloat16 [8, 2, 32, 8, 128], P('groups', None, 'dom', 'tp'), parts along dimension 0, may hold values from -8 to 8
- ancestors: int32 [8, 32], P('groups'), parts along dimension 0, may hold values from 0 to 31, as said below
- lengths: int32 [64], P('groups'), parts along dimension 0, may hold values from 1 to 12, as said below
Outputs:
- attended: bfloat16 [8, 32, 8, 8, 128], P('groups', 'dom', 'tp'), parts along dimension 0
There are 2 independent parts, one for each index of `groups`. A program takes and returns all parts, laid end to end along the dimension named above; each array names one. Nothing has to cross between parts.
Inputs may be any that keep to these rules, and one draw needn't show every extreme that they name: `ancestors`: particle p is owned by owner p // 16. In every step, of the 16 offspring of one owner at most 16 have their ancestor among the particles of any one owner, and each owner has exactly 16 from some one owner. `lengths`: the largest length is reached in every draw.
All inputs are finite; a program needn't handle non-finite values.
Results may differ from a plain program's by a relative error of at most 0.005.
Values may be sent and summed in bfloat16 or wider, within the bound.
A program may use at most 128 MiB of HBM per device.

v0:
```python
import functools
import math

import jax
import jax.numpy as jnp
from jax import lax
from jax.experimental import pallas as pl
from jax.experimental.pallas import tpu as pltpu
from jax.sharding import PartitionSpec as P

MESH = pl.DeviceIdType.MESH
SG = 2
CS = 2
AHEAD = 2
D_FOLD, D_SWAP = 2, 5
F32, BF16 = jnp.float32, jnp.bfloat16


def log2_int(n):
    assert n & (n - 1) == 0
    return n.bit_length() - 1


def nt(a, b):
    return lax.dot_general(a, b, (((1,), (1,)), ((), ())), preferred_element_type=F32)


def nn(a, b):
    return jnp.dot(a, b, preferred_element_type=F32)


def iota(shape, dim):
    return lax.broadcasted_iota(jnp.int32, shape, dim)


def kernel(
    n_ctx, owners, suf_dev, score_mul,
    q_ref, prompt_hbm, suf_hbm, new_hbm, anc_ref, len_ref, out_ref,
    raw, kf, vf, kh, vth, kx, vx, s_scr,
    suf_g, new_g, sfk, sfv, nfk, nfv, mask,
    acc, stat, msg, got_out, got_in, gst_out, gst_in, fin,
    load_sem, ex_local, ex_send, ex_recv,
    rs_send, rs_recv_out, rs_recv_in, ag_send, ag_recv,
):
    steps, per, heads, group, hd = q_ref.shape
    particles = per * owners
    prompt = kh.shape[0]
    rows = SG * per * group
    groups_of_steps = steps // SG
    nb = heads * groups_of_steps
    cuts = SG // CS
    width = CS * per * group
    lo, hi = n_ctx // 2 - 1, n_ctx // 2
    z = lax.axis_index("ctx")
    me = lax.axis_index("dom")
    n_suf = particles * suf_dev
    shares = n_ctx // steps
    chunk = per // shares
    n_new = owners * chunk
    n_ext = mask.shape[1]
    my_step = z // shares
    p0 = lax.rem(z, shares) * chunk

    loads = [
        pltpu.make_async_copy(prompt_hbm.at[i], raw.at[i], load_sem.at[i]) for i in range(2)
    ]
    for c in loads:
        c.start()

    barrier = pltpu.get_barrier_semaphore()
    for d in range(1, owners):
        pl.semaphore_signal(
            barrier, inc=1, device_id={"dom": lax.rem(me + d, owners)}, device_id_type=MESH
        )

    @pl.when(z > 0)
    def _():
        pl.semaphore_signal(barrier, inc=1, device_id={"ctx": z - 1}, device_id_type=MESH)

    @pl.when(z < n_ctx - 1)
    def _():
        pl.semaphore_signal(barrier, inc=1, device_id={"ctx": z + 1}, device_id_type=MESH)

    expected = (owners - 1) + jnp.where(z > 0, 1, 0) + jnp.where(z < n_ctx - 1, 1, 0)
    pl.semaphore_wait(barrier, expected)

    if shares == 1:
        new_src = new_hbm.at[my_step]
    else:
        new_src = new_hbm.at[
            my_step, :, pl.ds(pl.multiple_of(p0 * heads, chunk * heads), chunk * heads), :
        ]
    exchange = []
    for d in range(1, owners):
        peer = {"dom": lax.rem(me + d, owners)}
        for i, (src, dst) in enumerate(((suf_hbm, suf_g), (new_src, new_g))):
            exchange.append(
                pltpu.make_async_remote_copy(
                    src_ref=src, dst_ref=dst.at[me],
                    send_sem=ex_send.at[i, d - 1], recv_sem=ex_recv.at[i, d - 1],
                    device_id=peer, device_id_type=MESH,
                )
            )
    own = [
        pltpu.make_async_copy(suf_hbm, suf_g.at[me], ex_local.at[0]),
        pltpu.make_async_copy(new_src, new_g.at[me], ex_local.at[1]),
    ]
    for c in exchange + own:
        c.start()

    key = iota((n_ext, particles), 0)
    col = iota((n_ext, particles), 1)
    suf_particle = key >> log2_int(suf_dev)
    suf_pos = (key & (suf_dev - 1)) + z * suf_dev
    reach = (key < n_suf) & (suf_particle == col) & (suf_pos < len_ref[...])
    state = jnp.where(reach, 1.0, 0.0)
    rest = key - n_suf
    new_particle = (rest >> log2_int(chunk)) * per + (rest & (chunk - 1)) + p0
    is_new = jnp.where(
        (rest >= 0) & (rest < n_new) & (new_particle == col), 1.0, 0.0
    )
    spread = jnp.where(
        iota((particles, per * group), 0)
        == (iota((particles, per * group), 1) >> log2_int(group)) + me * per,
        1.0, 0.0,
    ).astype(BF16)
    for s in range(steps):
        parents = anc_ref[pl.ds(s, 1), :]
        move = jnp.where(iota((particles, particles), 0) == parents, 1.0, 0.0).astype(BF16)
        state = nn(state.astype(BF16), move)
        state = state + is_new * jnp.where(my_step == s, 1.0, 0.0)
        wide = nn(state.astype(BF16), spread)
        mask[s] = jnp.where(wide > 0.5, 0.0, -1e30)

    for src, dst in ((0, kf), (1, vf)):
        loads[src].wait()
        size = 1024

        def widen(i, _, src=src, dst=dst):
            at = pl.ds(pl.multiple_of(i * size, size), size)
            dst[at, :] = raw[src, at, :].astype(F32)
            return 0

        lax.fori_loop(0, raw.shape[1] // size, widen, 0)

    def parts(b):
        h = b // groups_of_steps
        return h, (b - h * groups_of_steps) * SG

    def queries_of(b):
        h, s0 = parts(b)
        out = [
            q_ref[s0 + i, :, h].astype(F32).reshape(per * group, hd) for i in range(SG)
        ]
        return jnp.concatenate(out, axis=0).astype(BF16)

    def extra_rows(suf, new, h):
        pieces = [suf[pl.ds(h, n_suf, stride=heads), :], new[pl.ds(h, n_new, stride=heads), :]]
        if n_ext > n_suf + n_new:
            pieces.append(jnp.zeros((n_ext - n_suf - n_new, hd), F32))
        return jnp.concatenate(pieces, axis=0)

    def bias_of(s0):
        return jnp.concatenate([mask[s0 + i] for i in range(SG)], axis=1)

    def prompt_stage(b, extra):
        h, s0 = parts(b)

        @pl.when(s0 == 0)
        def _():
            size = 256
            for i in range(prompt // size):
                at = pl.ds(h + i * size * heads, size, stride=heads)
                kh[pl.ds(i * size, size), :] = kf[at, :].astype(BF16)
                vth[:, pl.ds(i * size, size)] = vf[at, :].T.astype(BF16)
            if extra:
                kx[...] = extra_rows(sfk, nfk, h).astype(BF16)
                vx[...] = extra_rows(sfv, nfv, h).T.astype(BF16)

        q = queries_of(b)
        size = 512
        top = None
        if extra:
            sx = nt(kx[...], q) * score_mul + bias_of(s0)
        for i in range(prompt // size):
            at = pl.ds(i * size, size)
            s = nt(kh[at, :], q)
            s_scr[at, :] = s
            t = jnp.max(s, axis=0, keepdims=True)
            top = t if top is None else jnp.maximum(top, t)
        top = top * score_mul
        total = jnp.zeros((1, rows), F32)
        numer = jnp.zeros((hd, rows), F32)
        if extra:
            top = jnp.maximum(top, jnp.max(sx, axis=0, keepdims=True))
            w = jnp.exp2(sx - top)
            total += jnp.sum(w, axis=0, keepdims=True)
            numer += nn(vx[...], w.astype(BF16))
        for i in range(prompt // size):
            at = pl.ds(i * size, size)
            w = jnp.exp2(s_scr[at, :] * score_mul - top)
            total += jnp.sum(w, axis=0, keepdims=True)
            numer += nn(vth[:, at], w.astype(BF16))
        put(b, top, total, numer, extra)
        if extra:
            start_inward(b)

    def put(b, top, total, numer, ready):
        small = jnp.where(iota((2, rows), 0) == 0, top, total)
        for i in range(cuts):
            at = slice(i * width, (i + 1) * width)
            stat[b * cuts + i] = small[:, at]
            acc[b * cuts + i] = numer[:, at]
            if ready:
                msg[b * cuts + i] = numer[:, at].astype(BF16)

    def unpack_extra():
        for c in own:
            c.wait()
        for c in exchange:
            c.wait()
        ps, pn = suf_g.shape[2], new_g.shape[2]
        for o in range(owners):
            for i, dst in enumerate((sfk, sfv)):
                dst[pl.ds(o * ps, ps), :] = suf_g[o, i].astype(F32)
            for i, dst in enumerate((nfk, nfv)):
                dst[pl.ds(o * pn, pn), :] = new_g[o, i].astype(F32)

    def local_stage(b):
        h, s0 = parts(b)
        ks = extra_rows(sfk, nfk, h).astype(BF16)
        vt = extra_rows(sfv, nfv, h).T.astype(BF16)
        s = nt(ks, queries_of(b)) * score_mul + bias_of(s0)
        small = jnp.concatenate([stat[b * cuts + i] for i in range(cuts)], axis=1)
        old_numer = jnp.concatenate([acc[b * cuts + i] for i in range(cuts)], axis=1)
        old_top, old_total = small[0:1], small[1:2]
        new_top = jnp.maximum(old_top, jnp.max(s, axis=0, keepdims=True))
        w = jnp.exp2(s - new_top)
        keep = jnp.exp2(old_top - new_top)
        total = old_total * keep + jnp.sum(w, axis=0, keepdims=True)
        numer = old_numer * keep + nn(vt, w.astype(BF16))
        put(b, new_top, total, numer, True)
        start_inward(b)

    mid = (z == lo) | (z == hi)
    left_half = z <= lo
    inner = jnp.where(left_half, z + 1, z - 1)
    outer = jnp.where(left_half, z - 1, z + 1)
    has_outer = (z > 0) & (z < n_ctx - 1)

    def inward(c, across):
        data, small, sems = (
            (got_in, gst_in, rs_recv_in) if across else (got_out, gst_out, rs_recv_out)
        )
        return [
            pltpu.make_async_remote_copy(
                src_ref=src.at[c], dst_ref=dst.at[c],
                send_sem=rs_send.at[i, c], recv_sem=sems.at[i, c],
                device_id={"ctx": inner}, device_id_type=MESH,
            )
            for i, (src, dst) in enumerate(((stat, small), (msg, data)))
        ]

    def outward(c):
        return pltpu.make_async_remote_copy(
            src_ref=fin.at[c], dst_ref=fin.at[c],
            send_sem=ag_send.at[c], recv_sem=ag_recv.at[c],
            device_id={"ctx": outer}, device_id_type=MESH,
        )

    def start_inward(b):
        @pl.when(jnp.logical_not(has_outer))
        def _():
            for i in range(cuts):
                send(b * cuts + i)

    def send(c):
        for across in (True, False):
            @pl.when(mid if across else jnp.logical_not(mid))
            def _(across=across):
                for copy in inward(c, across):
                    copy.start()

    def merge(first, second):
        m1, l1, a1 = first
        m2, l2, a2 = second
        m = jnp.maximum(m1, m2)
        c1, c2 = jnp.exp2(m1 - m), jnp.exp2(m2 - m)
        return m, l1 * c1 + l2 * c2, a1 * c1 + a2 * c2

    def fold_stage(c):
        @pl.when(has_outer)
        def _():
            for copy in inward(c, False):
                copy.wait_recv()
            top, total, numer = merge(
                (stat[c, 0:1, :], stat[c, 1:2, :], acc[c]),
                (gst_out[c, 0:1, :], gst_out[c, 1:2, :], got_out[c].astype(F32)),
            )
            stat[c] = jnp.where(iota((2, width), 0) == 0, top, total)
            msg[c] = numer.astype(BF16)
            send(c)

    def put_out(c):
        h = c // (groups_of_steps * cuts)
        s0 = (c - h * (groups_of_steps * cuts)) * CS
        for i in range(CS):
            out_ref[s0 + i, :, h] = fin[c, i]

    def swap_stage(c):
        @pl.when(mid)
        def _():
            for copy in inward(c, True):
                copy.wait_recv()
            mine = (stat[c], msg[c].astype(F32))
            theirs = (gst_in[c], got_in[c].astype(F32))
            low = [jnp.where(left_half, a, b) for a, b in zip(mine, theirs)]
            high = [jnp.where(left_half, b, a) for a, b in zip(mine, theirs)]
            _, total, numer = merge(
                (low[0][0:1], low[0][1:2], low[1]), (high[0][0:1], high[0][1:2], high[1])
            )
            done = numer / total
            for i in range(CS):
                wide = done[:, i * per * group:(i + 1) * per * group].T
                fin[c, i] = wide.reshape(per, group, hd).astype(BF16)

            @pl.when(has_outer)
            def _():
                outward(c).start()

            put_out(c)

    def spread_stage(c):
        @pl.when(jnp.logical_not(mid))
        def _():
            outward(c).wait_recv()

            @pl.when(has_outer)
            def _():
                outward(c).start()

            put_out(c)

        for across in (True, False):
            @pl.when(mid if across else jnp.logical_not(mid))
            def _(across=across):
                for copy in inward(c, across):
                    copy.wait_send()

        @pl.when(has_outer)
        def _():
            outward(c).wait_send()

    def each(stage, b):
        for i in range(cuts):
            stage(b * cuts + i)

    def run(i, _):
        @pl.when(i < AHEAD)
        def _():
            prompt_stage(i, False)

        @pl.when(i == AHEAD)
        def _():
            unpack_extra()

            def add(b, _):
                local_stage(b)
                return 0

            lax.fori_loop(0, AHEAD, add, 0)

        @pl.when((i >= AHEAD) & (i < nb))
        def _():
            prompt_stage(i, True)

        for delay, stage in ((D_FOLD, fold_stage), (D_SWAP, swap_stage)):
            @pl.when((i >= delay) & (i < nb + delay))
            def _(delay=delay, stage=stage):
                each(stage, i - delay)
        return 0

    lax.fori_loop(0, nb + D_SWAP, run, 0)

    def close(c, _):
        spread_stage(c)
        return 0

    lax.fori_loop(0, nb * cuts, close, 0)


def on_device(n_ctx, owners, queries, prompt_cache, suffix_cache, new_kv, ancestors, lengths):
    steps, per, heads, group, hd = queries.shape
    prompt = prompt_cache.shape[1]
    suf_dev = suffix_cache.shape[2]
    particles = ancestors.shape[1]
    rows = SG * per * group
    nc = heads * (steps // CS)
    width = CS * per * group
    shares = n_ctx // steps
    chunk = per // shares
    n_ext = -(-(particles * suf_dev + owners * chunk) // 128) * 128
    dma = pltpu.SemaphoreType.DMA
    score_mul = math.log2(math.e) / math.sqrt(hd)
    ps, pn = per * suf_dev * heads, chunk * heads
    any_spec = pl.BlockSpec(memory_space=pl.ANY)
    vmem_spec = pl.BlockSpec(memory_space=pltpu.VMEM)
    return pl.pallas_call(
        functools.partial(kernel, n_ctx, owners, suf_dev, score_mul),
        out_shape=jax.ShapeDtypeStruct(queries.shape, BF16),
        in_specs=[vmem_spec, any_spec, any_spec, any_spec, vmem_spec, vmem_spec],
        out_specs=vmem_spec,
        scratch_shapes=[
            pltpu.VMEM((2, prompt * heads, hd), BF16),
            pltpu.VMEM((prompt * heads, hd), F32),
            pltpu.VMEM((prompt * heads, hd), F32),
            pltpu.VMEM((prompt, hd), BF16),
            pltpu.VMEM((hd, prompt), BF16),
            pltpu.VMEM((n_ext, hd), BF16),
            pltpu.VMEM((hd, n_ext), BF16),
            pltpu.VMEM((prompt, rows), F32),
            pltpu.VMEM((owners, 2, ps, hd), BF16),
            pltpu.VMEM((owners, 2, pn, hd), BF16),
            pltpu.VMEM((owners * ps, hd), F32),
            pltpu.VMEM((owners * ps, hd), F32),
            pltpu.VMEM((owners * pn, hd), F32),
            pltpu.VMEM((owners * pn, hd), F32),
            pltpu.VMEM((steps, n_ext, per * group), F32),
            pltpu.VMEM((nc, hd, width), F32),
            pltpu.VMEM((nc, 2, width), F32),
            pltpu.VMEM((nc, hd, width), BF16),
            pltpu.VMEM((nc, hd, width), BF16),
            pltpu.VMEM((nc, hd, width), BF16),
            pltpu.VMEM((nc, 2, width), F32),
            pltpu.VMEM((nc, 2, width), F32),
            pltpu.VMEM((nc, CS, per, group, hd), BF16),
            dma((2,)),
            dma((2,)),
            dma((2, max(owners - 1, 1))),
            dma((2, max(owners - 1, 1))),
            dma((2, nc)),
            dma((2, nc)),
            dma((2, nc)),
            dma((nc,)),
            dma((nc,)),
        ],
        compiler_params=pltpu.CompilerParams(
            collective_id=0, has_side_effects=True, vmem_limit_bytes=60 << 20
        ),
    )(
        queries,
        prompt_cache.reshape(2, prompt * heads, hd),
        suffix_cache.reshape(2, ps, hd),
        new_kv.reshape(steps, 2, per * heads, hd),
        ancestors,
        lengths.reshape(1, particles),
    )


def solution(mesh):
    return jax.shard_map(
        functools.partial(on_device, mesh.shape["ctx"], mesh.shape["dom"]),
        mesh=mesh,
        in_specs=(
            P("groups", "dom", "tp", None, None),
            P("groups", "ctx", "tp", None),
            P("groups", "dom", "ctx", "tp", None),
            P("groups", None, "dom", "tp", None),
            P("groups", None),
            P("groups"),
        ),
        out_specs=P("groups", "dom", "tp", None, None),
        check_vma=False,
    )
```

profile of v0, /device:TPU:0, one launch (start us, length us, event | category | flops | bytes accessed | tf_op | source)
XLA Modules:
  0.0 34.3 jit_solution(4351513421367040353)
XLA Ops:
  0.0 32.5 %shard_map.64 = bf16[4,16,4,8,128]{4,3,2,1,0:T(8,128)(2,1)} custom-call(bf16[4,16,4,8,128]{4,3,2,1,0:T(8,128)(2,1)} %q_ref.1, bf16[2,8192,128]{2,1,0:T(8,128)(2,1)} %bitcast.4, bf16[2,256,128]{2,1,0:T(8,128)(2,1)} %bitcast.5, bf16[4,2,64,128]{3,2,1,0:T(8,128)(2,1)} %bitcast.6, s32[4,32]{1,0:T(4,128)} %anc_ref.1, s32[1,32]{1,0:T(1,128)} %bitcast.7), custom_call_target="tpu_custom_call" | custom-call | tf_op jit(solution)/shard_map/pallas_call | solution.py:408
  32.5 1.9 %copy.8 = bf16[4,16,4,8,128]{4,3,2,1,0:T(8,128)(2,1)} copy(bf16[4,16,4,8,128]{4,3,2,1,0:T(8,128)(2,1)} %shard_map.64) | data formatting | bytes 1048576
where the time goes:
time: 34.5 us; the launch traced here: 34.3 us
  Pallas kernels  32.5 us (94%)
  local copies, waits for them, and re-layouts  1.87 us (5%)
    pallas_call x1, Pallas kernels, on_device(): pl.pallas_call(functools.partial(kernel, n_ctx, owners, suf_dev, score_mu...  32.5 us
    unnamed x1, local copies, waits for them, and re-layouts  1.87 us

commit v1 on v0

--- a/solution.py
+++ b/solution.py
@@ -35,11 +35,12 @@
 
 def kernel(
     n_ctx, owners, suf_dev, score_mul,
-    q_ref, prompt_hbm, suf_hbm, new_hbm, anc_ref, len_ref, out_ref,
+    q_hbm, prompt_hbm, suf_hbm, new_hbm, anc_hbm, len_hbm, out_ref,
+    q_ref, anc_ref, len_ref,
     raw, kf, vf, kh, vth, kx, vx, s_scr,
     suf_g, new_g, sfk, sfv, nfk, nfv, mask,
     acc, stat, msg, got_out, got_in, gst_out, gst_in, fin,
-    load_sem, ex_local, ex_send, ex_recv,
+    load_sem, small_sem, ex_local, ex_send, ex_recv,
     rs_send, rs_recv_out, rs_recv_in, ag_send, ag_recv,
 ):
     steps, per, heads, group, hd = q_ref.shape
@@ -64,7 +65,11 @@
     loads = [
         pltpu.make_async_copy(prompt_hbm.at[i], raw.at[i], load_sem.at[i]) for i in range(2)
     ]
-    for c in loads:
+    small = [
+        pltpu.make_async_copy(src, dst, small_sem.at[i])
+        for i, (src, dst) in enumerate(((anc_hbm, anc_ref), (len_hbm, len_ref), (q_hbm, q_ref)))
+    ]
+    for c in small[:2] + loads + small[2:]:
         c.start()
 
     barrier = pltpu.get_barrier_semaphore()
@@ -108,6 +113,8 @@
     for c in exchange + own:
         c.start()
 
+    for c in small[:2]:
+        c.wait()
     key = iota((n_ext, particles), 0)
     col = iota((n_ext, particles), 1)
     suf_particle = key >> log2_int(suf_dev)
@@ -142,6 +149,8 @@
             return 0
 
         lax.fori_loop(0, raw.shape[1] // size, widen, 0)
+
+    small[2].wait()
 
     def parts(b):
         h = b // groups_of_steps
@@ -407,10 +416,13 @@
     vmem_spec = pl.BlockSpec(memory_space=pltpu.VMEM)
     return pl.pallas_call(
         functools.partial(kernel, n_ctx, owners, suf_dev, score_mul),
-        out_shape=jax.ShapeDtypeStruct(queries.shape, BF16),
-        in_specs=[vmem_spec, any_spec, any_spec, any_spec, vmem_spec, vmem_spec],
+        out_shape=pltpu.VMEM(queries.shape, BF16),
+        in_specs=[any_spec] * 6,
         out_specs=vmem_spec,
         scratch_shapes=[
+            pltpu.VMEM(queries.shape, BF16),
+            pltpu.VMEM(ancestors.shape, jnp.int32),
+            pltpu.VMEM((1, particles), jnp.int32),
             pltpu.VMEM((2, prompt * heads, hd), BF16),
             pltpu.VMEM((prompt * heads, hd), F32),
             pltpu.VMEM((prompt * heads, hd), F32),
@@ -435,6 +447,7 @@
             pltpu.VMEM((nc, 2, width), F32),
             pltpu.VMEM((nc, CS, per, group, hd), BF16),
             dma((2,)),
+            dma((3,)),
             dma((2,)),
             dma((2, max(owners - 1, 1))),
             dma((2, max(owners - 1, 1))),
@@ -445,7 +458,7 @@
             dma((nc,)),
         ],
         compiler_params=pltpu.CompilerParams(
-            collective_id=0, has_side_effects=True, vmem_limit_bytes=60 << 20
+            collective_id=0, has_side_effects=True, vmem_limit_bytes=58 << 20
         ),
     )(
         queries,

time: 34.5 us -> 31.6 us (0.916)
  Pallas kernels: 32.5 us -> 30.6 us
  local copies, waits for them, and re-layouts: 1.87 us -> 0.8 us
    pallas_call x1, Pallas kernels: 32.5 us -> 30.6 us  [on_device(): pl.pallas_call(functools.partial(kernel, n_ctx, owners, suf_dev, score_mu...]
    unnamed x1, local copies, waits for them, and re-layouts: 1.87 us -> 0.8 us
where the time goes in v1:
time: 31.6 us; the launch traced here: 31.4 us
  Pallas kernels  30.6 us (97%)
  local copies, waits for them, and re-layouts  0.8 us (3%)
    pallas_call x1, Pallas kernels, on_device(): pl.pallas_call(functools.partial(kernel, n_ctx, owners, suf_dev, score_mu...  30.6 us
    unnamed x1, local copies, waits for them, and re-layouts  0.8 us

profile of v1, /device:TPU:0, one launch (start us, length us, event | category | flops | bytes accessed | tf_op | source)
XLA Modules:
  0.0 31.4 jit_solution(8075371657501737731)
XLA Ops:
  0.0 30.6 %shard_map.64 = bf16[4,16,4,8,128]{4,3,2,1,0:T(8,128)(2,1)S(1)} custom-call(bf16[4,16,4,8,128]{4,3,2,1,0:T(8,128)(2,1)} %q_hbm.1, bf16[2,8192,128]{2,1,0:T(8,128)(2,1)} %bitcast.4, bf16[2,256,128]{2,1,0:T(8,128)(2,1)} %bitcast.5, bf16[4,2,64,128]{3,2,1,0:T(8,128)(2,1)} %bitcast.6, s32[4,32]{1,0:T(4,128)} %anc_hbm.1, s32[1,32]{1,0:T(1,128)} %bitcast.7), custom_call_target="tpu_custom_call" | custom-call | tf_op jit(solution)/shard_map/pallas_call | solution.py:417
  30.6 0.8 %copy.8 = bf16[4,16,4,8,128]{4,3,2,1,0:T(8,128)(2,1)} copy(bf16[4,16,4,8,128]{4,3,2,1,0:T(8,128)(2,1)S(1)} %shard_map.64) | data formatting | bytes 1048576

commit v2 on v1

v2 whole, which is shorter than its diff:
```python
import functools
import math

import jax
import jax.numpy as jnp
from jax import lax
from jax.experimental import pallas as pl
from jax.experimental.pallas import tpu as pltpu
from jax.sharding import PartitionSpec as P

MESH = pl.DeviceIdType.MESH
SG = 2
PIECES = 4
TILE = 256
FOLD_LEFT, FOLD_RIGHT = 2, 2
SWAP_LEFT, SWAP_RIGHT = 5, 2
MASKED = -1e30
F32, BF16 = jnp.float32, jnp.bfloat16


def log2_int(n):
    assert n & (n - 1) == 0
    return n.bit_length() - 1


def nt(a, b):
    return lax.dot_general(a, b, (((1,), (1,)), ((), ())), preferred_element_type=F32)


def nn(a, b):
    return jnp.dot(a, b, preferred_element_type=F32)


def iota(shape, dim):
    return lax.broadcasted_iota(jnp.int32, shape, dim)


def kernel(
    n_ctx, owners, suf_dev, score_mul,
    q_hbm, prompt_hbm, suf_hbm, new_hbm, anc_hbm, len_hbm, out_ref,
    q_ref, anc_ref, len_ref, raw, kf, vf, kx, vx, s_scr, lse_scr,
    suf_g, new_g, sfk, sfv, nfk, nfv, mask,
    own, stat, msg, got_out, got_in, gst_out, gst_in,
    load_sem, small_sem, ex_local, ex_send, ex_recv,
    rs_send, rs_recv_out, rs_recv_in, ag_send, ag_recv,
):
    steps, per, heads, group, hd = q_ref.shape
    particles = per * owners
    prompt = kf.shape[0] // heads
    width = per * group
    rows = SG * width
    groups_of_steps = steps // SG
    nb = heads * groups_of_steps
    lo, hi = n_ctx // 2 - 1, n_ctx // 2
    z = lax.axis_index("ctx")
    me = lax.axis_index("dom")
    n_suf = particles * suf_dev
    shares = n_ctx // steps
    chunk = per // shares
    n_new = owners * chunk
    n_ext = mask.shape[2]
    my_step = z // shares
    p0 = lax.rem(z, shares) * chunk

    barrier = pltpu.get_barrier_semaphore()
    for d in range(1, owners):
        pl.semaphore_signal(
            barrier, inc=1, device_id={"dom": lax.rem(me + d, owners)}, device_id_type=MESH
        )

    @pl.when(z > 0)
    def _():
        pl.semaphore_signal(barrier, inc=1, device_id={"ctx": z - 1}, device_id_type=MESH)

    @pl.when(z < n_ctx - 1)
    def _():
        pl.semaphore_signal(barrier, inc=1, device_id={"ctx": z + 1}, device_id_type=MESH)

    piece = raw.shape[1] // PIECES
    loads = [
        [
            pltpu.make_async_copy(
                prompt_hbm.at[i, pl.ds(j * piece, piece)],
                raw.at[i, pl.ds(j * piece, piece)],
                load_sem.at[i, j],
            )
            for j in range(PIECES)
        ]
        for i in range(2)
    ]
    small = [
        pltpu.make_async_copy(src, dst, small_sem.at[i])
        for i, (src, dst) in enumerate(((anc_hbm, anc_ref), (len_hbm, len_ref), (q_hbm, q_ref)))
    ]
    for c in small[:2] + loads[0] + small[2:] + loads[1]:
        c.start()

    expected = (owners - 1) + jnp.where(z > 0, 1, 0) + jnp.where(z < n_ctx - 1, 1, 0)
    pl.semaphore_wait(barrier, expected)

    if shares == 1:
        new_src = new_hbm.at[my_step]
    else:
        new_src = new_hbm.at[
            my_step, :, pl.ds(pl.multiple_of(p0 * heads, chunk * heads), chunk * heads), :
        ]
    exchange = []
    for d in range(1, owners):
        peer = {"dom": lax.rem(me + d, owners)}
        for i, (src, dst) in enumerate(((suf_hbm, suf_g), (new_src, new_g))):
            exchange.append(
                pltpu.make_async_remote_copy(
                    src_ref=src, dst_ref=dst.at[me],
                    send_sem=ex_send.at[i, d - 1], recv_sem=ex_recv.at[i, d - 1],
                    device_id=peer, device_id_type=MESH,
                )
            )
    local = [
        pltpu.make_async_copy(suf_hbm, suf_g.at[me], ex_local.at[0]),
        pltpu.make_async_copy(new_src, new_g.at[me], ex_local.at[1]),
    ]
    for c in exchange + local:
        c.start()

    for c in small[:2]:
        c.wait()
    key = iota((n_ext, particles), 0)
    col = iota((n_ext, particles), 1)
    suf_particle = key >> log2_int(suf_dev)
    suf_pos = (key & (suf_dev - 1)) + z * suf_dev
    reach = (key < n_suf) & (suf_particle == col) & (suf_pos < len_ref[...])
    state = jnp.where(reach, 1.0, 0.0)
    rest = key - n_suf
    new_particle = (rest >> log2_int(chunk)) * per + (rest & (chunk - 1)) + p0
    is_new = jnp.where(
        (rest >= 0) & (rest < n_new) & (new_particle == col), 1.0, 0.0
    )
    spread = jnp.where(
        iota((width, particles), 1) == (iota((width, particles), 0) >> log2_int(group)) + me * per,
        1.0, 0.0,
    ).astype(BF16)
    for s in range(steps):
        parents = anc_ref[pl.ds(s, 1), :]
        move = jnp.where(iota((particles, particles), 0) == parents, 1.0, 0.0).astype(BF16)
        state = nn(state.astype(BF16), move)
        state = state + is_new * jnp.where(my_step == s, 1.0, 0.0)
        mask[s] = jnp.where(nt(spread, state.astype(BF16)) > 0.5, 0.0, MASKED)

    size = 1024
    for src, dst in ((0, kf), (1, vf)):
        for j in range(PIECES):
            loads[src][j].wait()

            def widen(i, _, src=src, dst=dst, j=j):
                at = pl.ds(pl.multiple_of(j * piece + i * size, size), size)
                dst[at, :] = raw[src, at, :].astype(F32)
                return 0

            lax.fori_loop(0, piece // size, widen, 0)

    small[2].wait()
    eye = iota((width, width), 0) == iota((width, width), 1)

    def parts(b):
        h = b // groups_of_steps
        return h, (b - h * groups_of_steps) * SG

    def to_lanes(x):
        return jnp.sum(jnp.where(eye, x, 0.0), axis=0, keepdims=True)

    def to_rows(x):
        return jnp.sum(jnp.where(eye, jnp.broadcast_to(x, eye.shape), 0.0), axis=1, keepdims=True)

    def head_tile(ref, h, i):
        return ref[pl.ds(h + i * TILE * heads, TILE, stride=heads), :].astype(BF16)

    def attend(b, use_prompt, use_extra):
        h, s0 = parts(b)
        q = jnp.concatenate(
            [q_ref[s0 + i, :, h].astype(F32).reshape(width, hd) for i in range(SG)], axis=0
        ).astype(BF16)
        tiles = []
        if use_prompt:
            for i in range(prompt // TILE):
                tiles.append((
                    i * TILE, TILE, None,
                    lambda i=i: head_tile(kf, h, i), lambda i=i: head_tile(vf, h, i),
                ))
        if use_extra:
            tiles.append((
                prompt, n_ext,
                lambda: jnp.concatenate([mask[s0 + i] for i in range(SG)], axis=0),
                lambda: kx[h], lambda: vx[h],
            ))
        peak = None
        for at, size, bias, keys, _ in tiles:
            score = nt(q, keys())
            if bias is not None:
                score = score + bias()
            s_scr[:, pl.ds(at, size)] = score
            for i in range(0, size, hd):
                part = score[:, i:i + hd]
                peak = part if peak is None else jnp.maximum(peak, part)
        peak = jnp.max(peak, axis=1, keepdims=True)
        both = None
        for at, size, _, _, values in tiles:
            w = jnp.exp2((s_scr[:, pl.ds(at, size)] - peak) * score_mul).astype(BF16)
            v = values()
            part = nn(w, jnp.concatenate([v, jnp.ones_like(v)], axis=1))
            both = part if both is None else both + part
        total = both[:, hd:]
        return both[:, :hd] / total, peak * score_mul + jnp.log2(total)

    def put(b, out, lse):
        for i in range(SG):
            c = b * SG + i
            at = slice(i * width, (i + 1) * width)
            own[c] = out[at]
            stat[c] = to_lanes(lse[at])

            @pl.when(jnp.logical_not(has_outer))
            def _(c=c, at=at):
                msg[c] = out[at].astype(BF16)
                send(c)

    def weight(first, second):
        top = jnp.maximum(first, second)
        e1, e2 = jnp.exp2(first - top), jnp.exp2(second - top)
        return e1 / (e1 + e2), top + jnp.log2(e1 + e2)

    def unpack_extra():
        for c in local:
            c.wait()
        for c in exchange:
            c.wait()
        ps, pn = suf_g.shape[2], new_g.shape[2]
        for o in range(owners):
            for i, dst in enumerate((sfk, sfv)):
                dst[pl.ds(o * ps, ps), :] = suf_g[o, i].astype(F32)
            for i, dst in enumerate((nfk, nfv)):
                dst[pl.ds(o * pn, pn), :] = new_g[o, i].astype(F32)
        for h in range(heads):
            for suf, new, dst in ((sfk, nfk, kx), (sfv, nfv, vx)):
                pieces = [
                    suf[pl.ds(h, n_suf, stride=heads), :], new[pl.ds(h, n_new, stride=heads), :]
                ]
                if n_ext > n_suf + n_new:
                    pieces.append(jnp.zeros((n_ext - n_suf - n_new, hd), F32))
                dst[h] = jnp.concatenate(pieces, axis=0).astype(BF16)

    mid = (z == lo) | (z == hi)
    left_half = z <= lo
    inner = jnp.where(left_half, z + 1, z - 1)
    outer = jnp.where(left_half, z - 1, z + 1)
    has_outer = (z > 0) & (z < n_ctx - 1)

    def inward(c, across):
        data, small_to, sems = (
            (got_in, gst_in, rs_recv_in) if across else (got_out, gst_out, rs_recv_out)
        )
        return [
            pltpu.make_async_remote_copy(
                src_ref=src.at[c], dst_ref=dst.at[c],
                send_sem=rs_send.at[i, c], recv_sem=sems.at[i, c],
                device_id={"ctx": inner}, device_id_type=MESH,
            )
            for i, (src, dst) in enumerate(((stat, small_to), (msg, data)))
        ]

    def place(c):
        h = c // steps
        return out_ref.at[c - h * steps, :, h]

    def outward(c):
        return pltpu.make_async_remote_copy(
            src_ref=place(c), dst_ref=place(c),
            send_sem=ag_send.at[c], recv_sem=ag_recv.at[c],
            device_id={"ctx": outer}, device_id_type=MESH,
        )

    def send(c):
        for across in (True, False):
            @pl.when(mid if across else jnp.logical_not(mid))
            def _(across=across):
                for copy in inward(c, across):
                    copy.start()

    def fold_stage(c):
        for copy in inward(c, False):
            copy.wait_recv()
        share, lse = weight(stat[c], gst_out[c])
        theirs = got_out[c].astype(F32)
        msg[c] = (theirs + to_rows(share) * (own[c] - theirs)).astype(BF16)
        stat[c] = lse
        send(c)

    def swap_stage(c):
        for copy in inward(c, True):
            copy.wait_recv()
        mine, theirs = (stat[c], msg[c].astype(F32)), (gst_in[c], got_in[c].astype(F32))
        low = [jnp.where(left_half, a, b) for a, b in zip(mine, theirs)]
        high = [jnp.where(left_half, b, a) for a, b in zip(mine, theirs)]
        share, _ = weight(low[0], high[0])
        done = high[1] + to_rows(share) * (low[1] - high[1])
        place(c)[...] = done.reshape(per, group, hd).astype(BF16)

        @pl.when(has_outer)
        def _():
            outward(c).start()

    def each(stage, b):
        for i in range(SG):
            stage(b * SG + i)

    out, lse = attend(0, True, False)
    own[pl.ds(0, SG)] = out.reshape(SG, width, hd)
    lse_scr[...] = lse
    unpack_extra()
    out_x, lse_x = attend(0, False, True)
    share, lse = weight(lse_scr[...], lse_x)
    put(0, out_x + share * (own[pl.ds(0, SG)].reshape(rows, hd) - out_x), lse)

    fold_delay = jnp.where(left_half, FOLD_LEFT, FOLD_RIGHT)
    swap_delay = jnp.where(left_half, SWAP_LEFT, SWAP_RIGHT)

    def run(i, _):
        @pl.when(i < nb)
        def _():
            put(i, *attend(i, True, True))

        for on, delay, stage in ((has_outer, fold_delay, fold_stage), (mid, swap_delay, swap_stage)):
            @pl.when(on & (i >= delay) & (i < nb + delay))
            def _(delay=delay, stage=stage):
                each(stage, i - delay)
        return 0

    lax.fori_loop(1, nb + max(FOLD_LEFT, FOLD_RIGHT, SWAP_LEFT, SWAP_RIGHT), run, 0)

    def close(c, _):
        @pl.when(jnp.logical_not(mid))
        def _():
            outward(c).wait_recv()

            @pl.when(has_outer)
            def _():
                outward(c).start()

        for across in (True, False):
            @pl.when(mid if across else jnp.logical_not(mid))
            def _(across=across):
                for copy in inward(c, across):
                    copy.wait_send()

        @pl.when(has_outer)
        def _():
            outward(c).wait_send()
        return 0

    lax.fori_loop(0, nb * SG, close, 0)


def on_device(n_ctx, owners, queries, prompt_cache, suffix_cache, new_kv, ancestors, lengths):
    steps, per, heads, group, hd = queries.shape
    prompt = prompt_cache.shape[1]
    suf_dev = suffix_cache.shape[2]
    particles = ancestors.shape[1]
    width = per * group
    rows = SG * width
    nc = heads * steps
    shares = n_ctx // steps
    chunk = per // shares
    n_ext = -(-(particles * suf_dev + owners * chunk) // 128) * 128
    dma = pltpu.SemaphoreType.DMA
    score_mul = math.log2(math.e) / math.sqrt(hd)
    ps, pn = per * suf_dev * heads, chunk * heads
    any_spec = pl.BlockSpec(memory_space=pl.ANY)
    vmem_spec = pl.BlockSpec(memory_space=pltpu.VMEM)
    return pl.pallas_call(
        functools.partial(kernel, n_ctx, owners, suf_dev, score_mul),
        out_shape=pltpu.VMEM(queries.shape, BF16),
        in_specs=[any_spec] * 6,
        out_specs=vmem_spec,
        scratch_shapes=[
            pltpu.VMEM(queries.shape, BF16),
            pltpu.VMEM(ancestors.shape, jnp.int32),
            pltpu.VMEM((1, particles), jnp.int32),
            pltpu.VMEM((2, prompt * heads, hd), BF16),
            pltpu.VMEM((prompt * heads, hd), F32),
            pltpu.VMEM((prompt * heads, hd), F32),
            pltpu.VMEM((heads, n_ext, hd), BF16),
            pltpu.VMEM((heads, n_ext, hd), BF16),
            pltpu.VMEM((rows, prompt + n_ext), F32),
            pltpu.VMEM((rows, hd), F32),
            pltpu.VMEM((owners, 2, ps, hd), BF16),
            pltpu.VMEM((owners, 2, pn, hd), BF16),
            pltpu.VMEM((owners * ps, hd), F32),
            pltpu.VMEM((owners * ps, hd), F32),
            pltpu.VMEM((owners * pn, hd), F32),
            pltpu.VMEM((owners * pn, hd), F32),
            pltpu.VMEM((steps, width, n_ext), F32),
            pltpu.VMEM((nc, width, hd), F32),
            pltpu.VMEM((nc, 1, width), F32),
            pltpu.VMEM((nc, width, hd), BF16),
            pltpu.VMEM((nc, width, hd), BF16),
            pltpu.VMEM((nc, width, hd), BF16),
            pltpu.VMEM((nc, 1, width), F32),
            pltpu.VMEM((nc, 1, width), F32),
            dma((2, PIECES)),
            dma((3,)),
            dma((2,)),
            dma((2, max(owners - 1, 1))),
            dma((2, max(owners - 1, 1))),
            dma((2, nc)),
            dma((2, nc)),
            dma((2, nc)),
            dma((nc,)),
            dma((nc,)),
        ],
        compiler_params=pltpu.CompilerParams(
            collective_id=0, has_side_effects=True, vmem_limit_bytes=58 << 20
        ),
    )(
        queries,
        prompt_cache.reshape(2, prompt * heads, hd),
        suffix_cache.reshape(2, ps, hd),
        new_kv.reshape(steps, 2, per * heads, hd),
        ancestors,
        lengths.reshape(1, particles),
    )


def solution(mesh):
    return jax.shard_map(
        functools.partial(on_device, mesh.shape["ctx"], mesh.shape["dom"]),
        mesh=mesh,
        in_specs=(
            P("groups", "dom", "tp", None, None),
            P("groups", "ctx", "tp", None),
            P("groups", "dom", "ctx", "tp", None),
            P("groups", None, "dom", "tp", None),
            P("groups", None),
            P("groups"),
        ),
        out_specs=P("groups", "dom", "tp", None, None),
        check_vma=False,
    )
```

time: 31.6 us -> 37.2 us (1.18)
  Pallas kernels: 30.6 us -> 36.3 us
    pallas_call x1, Pallas kernels: 30.6 us -> 36.3 us  [on_device(): pl.pallas_call(functools.partial(kernel, n_ctx, owners, suf_dev, score_mu...]
where the time goes in v2:
time: 37.2 us; the launch traced here: 37.1 us
  Pallas kernels  36.3 us (98%)
  local copies, waits for them, and re-layouts  0.8 us (2%)
    pallas_call x1, Pallas kernels, on_device(): pl.pallas_call(functools.partial(kernel, n_ctx, owners, suf_dev, score_mu...  36.3 us
    unnamed x1, local copies, waits for them, and re-layouts  0.8 us

profile of v2, /device:TPU:0, one launch (start us, length us, event | category | flops | bytes accessed | tf_op | source)
XLA Modules:
  0.0 37.1 jit_solution(366731208274781509)
XLA Ops:
  0.0 36.3 %shard_map.64 = bf16[4,16,4,8,128]{4,3,2,1,0:T(8,128)(2,1)S(1)} custom-call(bf16[4,16,4,8,128]{4,3,2,1,0:T(8,128)(2,1)} %q_hbm.1, bf16[2,8192,128]{2,1,0:T(8,128)(2,1)} %bitcast.4, bf16[2,256,128]{2,1,0:T(8,128)(2,1)} %bitcast.5, bf16[4,2,64,128]{3,2,1,0:T(8,128)(2,1)} %bitcast.6, s32[4,32]{1,0:T(4,128)} %anc_hbm.1, s32[1,32]{1,0:T(1,128)} %bitcast.7), custom_call_target="tpu_custom_call" | custom-call | tf_op jit(solution)/shard_map/pallas_call | solution.py:378
  36.3 0.8 %copy.8 = bf16[4,16,4,8,128]{4,3,2,1,0:T(8,128)(2,1)} copy(bf16[4,16,4,8,128]{4,3,2,1,0:T(8,128)(2,1)S(1)} %shard_map.64) | data formatting | bytes 1048576

commit v3 on v2

--- a/solution.py
+++ b/solution.py
@@ -38,7 +38,7 @@
 def kernel(
     n_ctx, owners, suf_dev, score_mul,
     q_hbm, prompt_hbm, suf_hbm, new_hbm, anc_hbm, len_hbm, out_ref,
-    q_ref, anc_ref, len_ref, raw, kf, vf, kx, vx, s_scr, lse_scr,
+    q_ref, anc_ref, len_ref, raw, kf, vf, kx, vx, s_scr, lse_scr, half_scr,
     suf_g, new_g, sfk, sfv, nfk, nfv, mask,
     own, stat, msg, got_out, got_in, gst_out, gst_in,
     load_sem, small_sem, ex_local, ex_send, ex_recv,
@@ -202,12 +202,16 @@
                 part = score[:, i:i + hd]
                 peak = part if peak is None else jnp.maximum(peak, part)
         peak = jnp.max(peak, axis=1, keepdims=True)
-        both = None
-        for at, size, _, _, values in tiles:
+        sums = [None, None]
+        for n, (at, size, _, _, values) in enumerate(tiles):
             w = jnp.exp2((s_scr[:, pl.ds(at, size)] - peak) * score_mul).astype(BF16)
             v = values()
             part = nn(w, jnp.concatenate([v, jnp.ones_like(v)], axis=1))
-            both = part if both is None else both + part
+            sums[n % 2] = part if sums[n % 2] is None else sums[n % 2] + part
+        both = sums[0]
+        if sums[1] is not None:
+            half_scr[...] = sums[1]
+            both = both + half_scr[...]
         total = both[:, hd:]
         return both[:, :hd] / total, peak * score_mul + jnp.log2(total)
 
@@ -391,6 +395,7 @@
             pltpu.VMEM((heads, n_ext, hd), BF16),
             pltpu.VMEM((rows, prompt + n_ext), F32),
             pltpu.VMEM((rows, hd), F32),
+            pltpu.VMEM((rows, 2 * hd), F32),
             pltpu.VMEM((owners, 2, ps, hd), BF16),
             pltpu.VMEM((owners, 2, pn, hd), BF16),
             pltpu.VMEM((owners * ps, hd), F32),

time: 37.2 us -> 35.6 us (0.957)
  Pallas kernels: 36.3 us -> 34.6 us
    pallas_call x1, Pallas kernels: 36.3 us -> 34.6 us  [on_device(): pl.pallas_call(functools.partial(kernel, n_ctx, owners, suf_dev, score_mu...]
where the time goes in v3:
time: 35.6 us; the launch traced here: 35.4 us
  Pallas kernels  34.6 us (97%)
  local copies, waits for them, and re-layouts  0.8 us (2%)
    pallas_call x1, Pallas kernels, on_device(): pl.pallas_call(functools.partial(kernel, n_ctx, owners, suf_dev, score_mu...  34.6 us
    unnamed x1, local copies, waits for them, and re-layouts  0.8 us

profile of v3, /device:TPU:0, one launch (start us, length us, event | category | flops | bytes accessed | tf_op | source)
XLA Modules:
  0.0 35.4 jit_solution(1638591300832425469)
XLA Ops:
  0.0 34.6 %shard_map.64 = bf16[4,16,4,8,128]{4,3,2,1,0:T(8,128)(2,1)S(1)} custom-call(bf16[4,16,4,8,128]{4,3,2,1,0:T(8,128)(2,1)} %q_hbm.1, bf16[2,8192,128]{2,1,0:T(8,128)(2,1)} %bitcast.4, bf16[2,256,128]{2,1,0:T(8,128)(2,1)} %bitcast.5, bf16[4,2,64,128]{3,2,1,0:T(8,128)(2,1)} %bitcast.6, s32[4,32]{1,0:T(4,128)} %anc_hbm.1, s32[1,32]{1,0:T(1,128)} %bitcast.7), custom_call_target="tpu_custom_call" | custom-call | tf_op jit(solution)/shard_map/pallas_call | solution.py:382
  34.6 0.8 %copy.8 = bf16[4,16,4,8,128]{4,3,2,1,0:T(8,128)(2,1)} copy(bf16[4,16,4,8,128]{4,3,2,1,0:T(8,128)(2,1)S(1)} %shard_map.64) | data formatting | bytes 1048576
